TPU v7x, 512 devices: a whole 4x8x8 slice. The times are simulated.
512 devices in a mesh: tm: 64 (over x, y, core), dp: 8 (over z).
Axes of the slice: x: 4, y: 8, z: 8, core: 2. Of those that a mesh axis runs over, the one named last changes fastest.
Arguments:
- frame_tokens: bfloat16 [8, 192, 64, 1280], P('dp', 'tm'), may hold values from -8 to 8
- visible: int32 [8, 192, 64], P('dp'), may hold values from 0 to 2
- grad_output: bfloat16 [8, 192, 64, 1280], P('dp', 'tm'), may hold values from -16 to 16
- norm_gain: float32 [1280], replicated, may hold values from 0.1 to 1.9
- query_weight: bfloat16 [1280, 640], P('tm'), may hold values from -1.5 to 1.5
- key_weight: bfloat16 [1280, 640], P('tm'), may hold values from -1.5 to 1.5
- value_weight: bfloat16 [1280, 640], P('tm'), may hold values from -0.15625 to 0.15625
- output_weight: bfloat16 [640, 1280], P('tm'), may hold values from -0.25 to 0.25
Outputs:
- block_out: bfloat16 [8, 192, 64, 1280], P('dp', 'tm')
- grad_tokens: bfloat16 [8, 192, 64, 1280], P('dp', 'tm')
- grad_output_weight: float32 [640, 1280], P('tm')
Inputs may be any that keep to these rules, and one draw needn't show every extreme that they name: visible[c, f, g] names which of the 3 cells of group g is visible in frame f.
All inputs are finite; a program needn't handle non-finite values.
Results may differ from a plain program's by a relative error of at most 0.012.
Values may be sent and summed in bfloat16 or wider, within the bound.
No kernel may reach another device: no remote copies, remote signals or barrier semaphores. Data moves between devices by JAX's collectives and lax.ppermute only.
A program may use at most 64 MiB of HBM per device.

v0:
```python
import math
import jax
import jax.numpy as jnp
from jax import lax
from jax.sharding import PartitionSpec as P

HEADS = 8
NORM_EPS = 1e-06


def normalize(token_rows, norm_gain):
    values = token_rows.astype(jnp.float32)
    centered = values - jnp.mean(values, axis=-1, keepdims=True)
    inverse = lax.rsqrt(jnp.mean(centered * centered, axis=-1, keepdims=True) + NORM_EPS)
    scaled = centered * inverse
    return (scaled, inverse, (scaled * norm_gain).astype(jnp.bfloat16))


def project(token_rows, weight):
    lead_shape = token_rows.shape[:-1]
    flat_rows = token_rows.reshape(-1, token_rows.shape[-1])
    result = jnp.dot(flat_rows, weight, preferred_element_type=jnp.float32)
    return result.astype(jnp.bfloat16).reshape(lead_shape + (weight.shape[1],))


def split_heads(values):
    return values.reshape(values.shape[:-1] + (HEADS, values.shape[-1] // HEADS))


def attend(query_rows, key_rows, value_rows, same_cell):
    score_scale = 1.0 / math.sqrt(query_rows.shape[-1] // HEADS)
    query_heads = split_heads(query_rows)
    key_heads = split_heads(key_rows)
    value_heads = split_heads(value_rows)
    scores = (
        jnp.einsum("fghe,tghe->ghft", query_heads, key_heads, preferred_element_type=jnp.float32)
        * score_scale
    )
    scores = jnp.where(same_cell[:, None], scores, -jnp.inf)
    row_top = jnp.max(scores, axis=-1, keepdims=True)
    expons = jnp.exp(scores - row_top)
    soft_probs = expons / jnp.sum(expons, axis=-1, keepdims=True)
    probs_low = soft_probs.astype(jnp.bfloat16)
    mixed_rows = jnp.einsum(
        "ghft,tghe->fghe", probs_low, value_heads, preferred_element_type=jnp.float32
    )
    return (soft_probs, probs_low, mixed_rows.reshape(query_rows.shape).astype(jnp.bfloat16))


def attend_back(query_rows, key_rows, value_rows, soft_probs, probs_low, grad_mixed):
    score_scale = 1.0 / math.sqrt(query_rows.shape[-1] // HEADS)
    query_heads = split_heads(query_rows)
    key_heads = split_heads(key_rows)
    value_heads = split_heads(value_rows)
    grad_heads = split_heads(grad_mixed)
    grad_probs = jnp.einsum(
        "fghe,tghe->ghft", grad_heads, value_heads, preferred_element_type=jnp.float32
    )
    centre = jnp.sum(soft_probs * grad_probs, axis=-1, keepdims=True)
    grad_scores = (soft_probs * (grad_probs - centre) * score_scale).astype(jnp.bfloat16)
    grad_query = jnp.einsum(
        "ghft,tghe->fghe", grad_scores, key_heads, preferred_element_type=jnp.float32
    )
    grad_key = jnp.einsum(
        "ghft,fghe->tghe", grad_scores, query_heads, preferred_element_type=jnp.float32
    )
    grad_value = jnp.einsum(
        "ghft,fghe->tghe", probs_low, grad_heads, preferred_element_type=jnp.float32
    )
    full_shape = query_rows.shape
    return (
        grad_query.reshape(full_shape).astype(jnp.bfloat16),
        grad_key.reshape(full_shape).astype(jnp.bfloat16),
        grad_value.reshape(full_shape).astype(jnp.bfloat16),
    )


def back_project(grad_query, grad_key, grad_value, query_weight, key_weight, value_weight):
    lead_shape = grad_query.shape[:-1]
    width = grad_query.shape[-1]
    total = jnp.dot(
        grad_query.reshape(-1, width), query_weight.T, preferred_element_type=jnp.float32
    )
    total = total + jnp.dot(
        grad_key.reshape(-1, width), key_weight.T, preferred_element_type=jnp.float32
    )
    total = total + jnp.dot(
        grad_value.reshape(-1, width), value_weight.T, preferred_element_type=jnp.float32
    )
    return total.astype(jnp.bfloat16).reshape(lead_shape + (query_weight.shape[0],))


def on_device(
    frame_tokens,
    visible,
    grad_output,
    norm_gain,
    query_weight,
    key_weight,
    value_weight,
    output_weight,
):
    query_weight, key_weight, value_weight, output_weight = (
        lax.all_gather(query_weight, "tm", axis=0, tiled=True),
        lax.all_gather(key_weight, "tm", axis=0, tiled=True),
        lax.all_gather(value_weight, "tm", axis=0, tiled=True),
        lax.all_gather(output_weight, "tm", axis=0, tiled=True),
    )
    shards = lax.axis_size("tm")
    tokens = frame_tokens[0]
    frame_count, visible_count, width = tokens.shape
    att_width = output_weight.shape[0]
    groups = visible_count // shards
    scaled, inverse, normed = normalize(tokens, norm_gain)
    local_cells = lax.dynamic_slice_in_dim(visible[0], lax.axis_index("tm") * groups, groups, 1)
    cell_major = local_cells.T
    same_cell = cell_major[:, :, None] == cell_major[:, None, :]
    query_rows = project(normed, query_weight)
    key_rows = project(normed, key_weight)
    value_rows = project(normed, value_weight)
    query_rows, key_rows, value_rows = (
        lax.all_to_all(query_rows, "tm", split_axis=1, concat_axis=0, tiled=True),
        lax.all_to_all(key_rows, "tm", split_axis=1, concat_axis=0, tiled=True),
        lax.all_to_all(value_rows, "tm", split_axis=1, concat_axis=0, tiled=True),
    )
    soft_probs, probs_low, mixed_cells = attend(query_rows, key_rows, value_rows, same_cell)
    mixed_frames = lax.all_to_all(mixed_cells, "tm", split_axis=0, concat_axis=1, tiled=True)
    flat_mixed = mixed_frames.reshape(-1, att_width)
    flat_tokens = tokens.reshape(-1, width)
    update = jnp.dot(flat_mixed, output_weight, preferred_element_type=jnp.float32)
    block_rows = (
        (flat_tokens.astype(jnp.float32) + update).astype(jnp.bfloat16).reshape(tokens.shape)
    )
    flat_grad = grad_output[0].reshape(-1, width)
    grad_mixed = jnp.dot(flat_grad, output_weight.T, preferred_element_type=jnp.float32)
    grad_mixed = grad_mixed.astype(jnp.bfloat16).reshape(frame_count, visible_count, att_width)
    term_share = lax.psum_scatter(
        jnp.dot(flat_mixed.T, flat_grad, preferred_element_type=jnp.float32),
        "tm",
        scatter_dimension=0,
        tiled=True,
    )
    grad_weight = lax.psum(term_share.astype(jnp.bfloat16), "dp").astype(jnp.float32)
    grad_cells = lax.all_to_all(grad_mixed, "tm", split_axis=1, concat_axis=0, tiled=True)
    grad_query, grad_key, grad_value = attend_back(
        query_rows, key_rows, value_rows, soft_probs, probs_low, grad_cells
    )
    grad_query, grad_key, grad_value = (
        lax.all_to_all(grad_query, "tm", split_axis=0, concat_axis=1, tiled=True),
        lax.all_to_all(grad_key, "tm", split_axis=0, concat_axis=1, tiled=True),
        lax.all_to_all(grad_value, "tm", split_axis=0, concat_axis=1, tiled=True),
    )
    grad_normed = back_project(
        grad_query, grad_key, grad_value, query_weight, key_weight, value_weight
    )
    weighted = grad_normed.astype(jnp.float32) * norm_gain
    first_mean = jnp.mean(weighted, axis=-1, keepdims=True)
    second_mean = jnp.mean(weighted * scaled, axis=-1, keepdims=True)
    grad_rows = inverse * (weighted - first_mean - scaled * second_mean) + grad_output[0].astype(
        jnp.float32
    )
    return (block_rows[None], grad_rows.astype(jnp.bfloat16)[None], grad_weight)


def solution(mesh):
    return jax.shard_map(
        on_device,
        mesh=mesh,
        in_specs=(
            P("dp", "tm", None, None),
            P("dp", None, None),
            P("dp", "tm", None, None),
            P(),
            P("tm", None),
            P("tm", None),
            P("tm", None),
            P("tm", None),
        ),
        out_specs=(P("dp", "tm", None, None), P("dp", "tm", None, None), P("tm", None)),
        check_vma=False,
    )
```

profile of v0, /device:TPU:64, one launch (start us, length us, event | category | flops | bytes accessed | tf_op | source)
XLA Modules:
  0.0 840.5 jit_solution(8921300924261810447)
XLA Ops:
  12.6 85.6 %all-gather.15.cloned.1.call-done = bf16[64,10,1280]{2,1,0:T(8,128)(2,1)} async-done(((bf16[1,10,1280]{2,1,0:T(8,128)(2,1)}), bf16[64,10,1280]{2,1,0:T(8,128)(2,1)}) %all-gather.15.cloned.1.call-update) | async-done | bytes 1638416 | tf_op jit(solution)/shard_map/all_gather | solution.py:107
  102.6 6.7 all-to-all-start.4
  110.7 71.2 %all-gather.13.cloned.1.call-done = bf16[64,20,640]{2,1,0:T(8,128)(2,1)} async-done(((bf16[1,20,640]{2,1,0:T(8,128)(2,1)}), bf16[64,20,640]{2,1,0:T(8,128)(2,1)}) %all-gather.13.cloned.1.call-update) | async-done | bytes 1638416 | tf_op jit(solution)/shard_map/all_gather | solution.py:105
  185.9 7.0 all-to-all-start.2
  192.9 72.7 %all-gather.11.cloned.1.call-done = bf16[64,20,640]{2,1,0:T(8,128)(2,1)} async-done(((bf16[1,20,640]{2,1,0:T(8,128)(2,1)}), bf16[64,20,640]{2,1,0:T(8,128)(2,1)}) %all-gather.11.cloned.1.call-update) | async-done | bytes 1638416 | tf_op jit(solution)/shard_map/all_gather | solution.py:104
  270.7 7.0 all-to-all-start.1
  277.8 71.5 %all-gather.9.cloned.1.call-done = bf16[64,20,640]{2,1,0:T(8,128)(2,1)} async-done(((bf16[1,20,640]{2,1,0:T(8,128)(2,1)}), bf16[64,20,640]{2,1,0:T(8,128)(2,1)}) %all-gather.9.cloned.1.call-update) | async-done | bytes 1638416 | tf_op jit(solution)/shard_map/all_gather | solution.py:106
  349.3 3.6 reshape.310
  364.3 7.0 all-to-all-start
  375.5 2.9 fusion.42
  387.9 10.7 %all-to-all-start.7 = ((bf16[64,2,960]{2,1,0:T(2,128)(2,1)}), bf16[64,2,960]{2,1,0:T(2,128)(2,1)}, u32[]{:S(2)}, u32[]{:S(2)}) async-start(bf16[64,2,960]{2,1,0:T(2,128)(2,1)} %reshape.328), calls=%async_computation.7 | async-start | bytes 524288 | tf_op jit(solution)/shard_map/all_to_all | solution.py:151
  411.6 10.5 %all-to-all-start.3 = ((bf16[64,2,960]{2,1,0:T(2,128)(2,1)}), bf16[64,2,960]{2,1,0:T(2,128)(2,1)}, u32[]{:S(2)}, u32[]{:S(2)}) async-start(bf16[64,2,960]{2,1,0:T(2,128)(2,1)} %reshape.322), calls=%async_computation.3 | async-start | bytes 524288 | tf_op jit(solution)/shard_map/all_to_all | solution.py:127
  424.7 4.3 fusion.19
  435.3 10.5 %all-to-all-start.6 = ((bf16[64,2,960]{2,1,0:T(2,128)(2,1)}), bf16[64,2,960]{2,1,0:T(2,128)(2,1)}, u32[]{:S(2)}, u32[]{:S(2)}) async-start(bf16[64,2,960]{2,1,0:T(2,128)(2,1)} %reshape.326), calls=%async_computation.6 | async-start | bytes 524288 | tf_op jit(solution)/shard_map/all_to_all | solution.py:150
  447.8 4.4 fusion.16
  461.3 3.1 reduce.12
  470.7 3.1 reduce.9
  477.2 10.5 %all-to-all-start.5 = ((bf16[64,2,960]{2,1,0:T(2,128)(2,1)}), bf16[64,2,960]{2,1,0:T(2,128)(2,1)}, u32[]{:S(2)}, u32[]{:S(2)}) async-start(bf16[64,2,960]{2,1,0:T(2,128)(2,1)} %reshape.324), calls=%async_computation.5 | async-start | bytes 524288 | tf_op jit(solution)/shard_map/all_to_all | solution.py:149
  487.7 2.9 reshape.327
  490.6 3.1 reduce.11
  497.1 3.0 fusion.2
  505.3 3.1 reduce.10
  514.9 287.3 %all-reduce.2 = bf16[640,1280]{1,0:T(8,128)(2,1)} all-reduce(f32[640,1280]{1,0:T(8,128)} %fusion.45), channel_id=2, replica_groups=mesh['tm'=64,'dp'=8] {'tm'}, use_global_device_ids=true, to_apply=%region_7.8.clone | all-reduce | flops 819200 | bytes 4915200
  803.0 29.0 %psum.7 = bf16[10,1280]{1,0:T(8,128)(2,1)S(1)} all-reduce(bf16[10,1280]{1,0:T(8,128)(2,1)S(1)} %dynamic-slice_convert_fusion), channel_id=1, replica_groups=mesh['tm'=64,'dp'=8] {'dp'}, use_global_device_ids=true, to_apply=%region_8.9 | all-reduce | flops 12800 | bytes 51200 | tf_op jit(solution)/shard_map/psum | solution.py:143
  (112 shorter events, 105.1 us)
Async XLA Ops:
  7.2 185.7 %copy-start = (s32[1,192,64]{1,2,0:T(8,128)S(1)}, s32[1,192,64]{1,2,0:T(8,128)}, u32[]{:S(2)}) copy-start(s32[1,192,64]{1,2,0:T(8,128)} %param.9) | copy-start | bytes 147460
  7.2 91.1 %all-gather.15.cloned.1.call-start = ((), (), s32[]{:S(2)}) async-start(), calls=%async_computation.11 | async-start | bytes 2662400 | tf_op jit(solution)/shard_map/all_gather | solution.py:107
  7.9 174.0 %all-gather.13.cloned.1.call-start = ((), (), s32[]{:S(2)}) async-start(), calls=%async_computation.10 | async-start | bytes 1996800 | tf_op jit(solution)/shard_map/all_gather | solution.py:105
  8.7 257.0 %all-gather.11.cloned.1.call-start = ((), (), s32[]{:S(2)}) async-start(), calls=%async_computation.9 | async-start | bytes 1996800 | tf_op jit(solution)/shard_map/all_gather | solution.py:104
  9.4 339.9 %all-gather.9.cloned.1.call-start = ((), (), s32[]{:S(2)}) async-start(), calls=%async_computation.8 | async-start | bytes 1996800 | tf_op jit(solution)/shard_map/all_gather | solution.py:106
  12.6 88.3 %copy-start.6 = (bf16[1,3,64,1280]{3,2,1,0:T(8,128)(2,1)S(1)}, bf16[1,3,64,1280]{3,2,1,0:T(8,128)(2,1)}, u32[]{:S(2)}) copy-start(bf16[1,3,64,1280]{3,2,1,0:T(8,128)(2,1)} %param.10) | copy-start | bytes 1474564
  101.0 8.4 copy-start.3
  101.0 8.4 copy-start.14
  102.6 83.2 %all-to-all-start.4 = ((bf16[3,64,640]{2,0,1:T(4,128)(2,1)}), bf16[3,64,640]{2,0,1:T(4,128)(2,1)S(1)}, u32[]{:S(2)}, u32[]{:S(2)}) async-start(bf16[3,64,640]{2,0,1:T(4,128)(2,1)} %copy.52), calls=%async_computation.4 | async-start | bytes 655360 | tf_op jit(solution)/shard_map/all_to_all | solution.py:144
  110.7 73.6 %copy-start.5 = (bf16[192,1280]{1,0:T(8,128)(2,1)}, bf16[192,1280]{1,0:T(8,128)(2,1)S(1)}, u32[]{:S(2)}) copy-start(bf16[192,1280]{1,0:T(8,128)(2,1)S(1)} %get-tuple-element.6) | copy-start | bytes 1474564
  185.9 7.1 copy-start.11
  185.9 84.8 %all-to-all-start.2 = ((bf16[3,64,640]{2,0,1:T(4,128)(2,1)}), bf16[3,64,640]{2,0,1:T(4,128)(2,1)}, u32[]{:S(2)}, u32[]{:S(2)}) async-start(bf16[3,64,640]{2,0,1:T(4,128)(2,1)} %copy.45), calls=%async_computation.2 | async-start | bytes 655360 | tf_op jit(solution)/shard_map/all_to_all | solution.py:123
  270.7 93.7 %all-to-all-start.1 = ((bf16[3,64,640]{2,0,1:T(4,128)(2,1)}), bf16[3,64,640]{2,0,1:T(4,128)(2,1)}, u32[]{:S(2)}, u32[]{:S(2)}) async-start(bf16[3,64,640]{2,0,1:T(4,128)(2,1)} %copy.44), calls=%async_computation.1 | async-start | bytes 655360 | tf_op jit(solution)/shard_map/all_to_all | solution.py:122
  364.3 23.6 %all-to-all-start = ((bf16[3,64,640]{2,0,1:T(4,128)(2,1)}), bf16[3,64,640]{2,0,1:T(4,128)(2,1)}, u32[]{:S(2)}, u32[]{:S(2)}) async-start(bf16[3,64,640]{2,0,1:T(4,128)(2,1)} %copy.43), calls=%async_computation | async-start | bytes 655360 | tf_op jit(solution)/shard_map/all_to_all | solution.py:124
  387.9 23.7 %all-to-all-start.7 = ((bf16[64,2,960]{2,1,0:T(2,128)(2,1)}), bf16[64,2,960]{2,1,0:T(2,128)(2,1)}, u32[]{:S(2)}, u32[]{:S(2)}) async-start(bf16[64,2,960]{2,1,0:T(2,128)(2,1)} %reshape.328), calls=%async_computation.7 | async-start | bytes 524288 | tf_op jit(solution)/shard_map/all_to_all | solution.py:151
  411.6 23.8 %all-to-all-start.3 = ((bf16[64,2,960]{2,1,0:T(2,128)(2,1)}), bf16[64,2,960]{2,1,0:T(2,128)(2,1)}, u32[]{:S(2)}, u32[]{:S(2)}) async-start(bf16[64,2,960]{2,1,0:T(2,128)(2,1)} %reshape.322), calls=%async_computation.3 | async-start | bytes 524288 | tf_op jit(solution)/shard_map/all_to_all | solution.py:127
  435.3 41.9 %all-to-all-start.6 = ((bf16[64,2,960]{2,1,0:T(2,128)(2,1)}), bf16[64,2,960]{2,1,0:T(2,128)(2,1)}, u32[]{:S(2)}, u32[]{:S(2)}) async-start(bf16[64,2,960]{2,1,0:T(2,128)(2,1)} %reshape.326), calls=%async_computation.6 | async-start | bytes 524288 | tf_op jit(solution)/shard_map/all_to_all | solution.py:150
  477.2 25.3 %all-to-all-start.5 = ((bf16[64,2,960]{2,1,0:T(2,128)(2,1)}), bf16[64,2,960]{2,1,0:T(2,128)(2,1)}, u32[]{:S(2)}, u32[]{:S(2)}) async-start(bf16[64,2,960]{2,1,0:T(2,128)(2,1)} %reshape.324), calls=%async_computation.5 | async-start | bytes 524288 | tf_op jit(solution)/shard_map/all_to_all | solution.py:149
  497.1 3.0 copy-start.7
  497.1 3.0 copy-start.10
  512.1 1.7 copy-start.9
  512.1 1.7 copy-start.12
  514.9 317.8 %copy-start.4 = (bf16[1,3,64,1280]{3,2,1,0:T(8,128)(2,1)S(1)}, bf16[1,3,64,1280]{3,2,1,0:T(8,128)(2,1)}, u32[]{:S(2)}) copy-start(bf16[1,3,64,1280]{3,2,1,0:T(8,128)(2,1)} %param.8) | copy-start | bytes 1474564
  514.9 317.8 %copy-start.8 = (bf16[1,3,64,1280]{3,2,1,0:T(8,128)(2,1)S(1)}, bf16[1,3,64,1280]{3,2,1,0:T(8,128)(2,1)}, u32[]{:S(2)}) copy-start(bf16[1,3,64,1280]{3,2,1,0:T(8,128)(2,1)} %param.10) | copy-start | bytes 1474564
  (3 other events, 4.0 us)
Sparse Core Ops, SparseCore 0:
  11.3 86.8 all-gather.14
  101.5 80.3 all-gather.12
  185.2 80.4 all-gather.10
  268.8 80.4 all-gather.8
where the time goes:
time: 843 us; the launch traced here: 840 us
  blocking collectives  316 us (37%)
  waiting for transfers between devices  304 us (36%)
  local copies, waits for them, and re-layouts  75.6 us (9%)
  starting transfers between devices  70.1 us (8%)
  matrix products  31.9 us (4%)
  other arithmetic  28.2 us (3%)
  between operations  14.7 us (2%)
    unnamed x1, blocking collectives  287 us
    all_gather x1, waiting for transfers between devices, on_device(): lax.all_gather(output_weight, 'tm', axis=0, tiled=True)  85.6 us
    all_gather x1, waiting for transfers between devices, on_device(): lax.all_gather(query_weight, 'tm', axis=0, tiled=True)  72.7 us
    all_gather x1, waiting for transfers between devices, on_device(): lax.all_gather(value_weight, 'tm', axis=0, tiled=True)  71.5 us
    all_gather x1, waiting for transfers between devices, on_device(): lax.all_gather(key_weight, 'tm', axis=0, tiled=True)  71.2 us
    unnamed x47, local copies, waits for them, and re-layouts  40.3 us
    psum x1, blocking collectives, on_device(): lax.psum(term_share.astype(jnp.bfloat16), 'dp').astype(jnp.float32)  29 us
  transfers between devices with their start and end apart: 12, of which 4 were waited for; matrix products, arithmetic and copies ran while one was open for 14% of the time, Pallas kernels for 0%

commit v1 on v0

--- a/solution.py
+++ b/solution.py
@@ -6,6 +6,11 @@
 
 HEADS = 8
 NORM_EPS = 1e-06
+
+
+def gather_and_add(x, name):
+    pieces = lax.all_gather(x, name)
+    return jnp.sum(pieces, axis=0)
 
 
 def normalize(token_rows, norm_gain):
@@ -140,7 +145,7 @@
         scatter_dimension=0,
         tiled=True,
     )
-    grad_weight = lax.psum(term_share.astype(jnp.bfloat16), "dp").astype(jnp.float32)
+    grad_weight = gather_and_add(term_share.astype(jnp.bfloat16), "dp").astype(jnp.float32)
     grad_cells = lax.all_to_all(grad_mixed, "tm", split_axis=1, concat_axis=0, tiled=True)
     grad_query, grad_key, grad_value = attend_back(
         query_rows, key_rows, value_rows, soft_probs, probs_low, grad_cells

time: 843 us -> 840 us (level)
    psum x1 -> x0, blocking collectives: 29 us -> none  [on_device(): lax.psum(term_share.astype(jnp.bfloat16), 'dp').astype(jnp.float32)]
    all_gather x0 -> x1, blocking collectives: none -> 26 us  [gather_and_add(): pieces = lax.all_gather(x, name)]
    unnamed x47 -> x48, local copies, waits for them, and re-layouts: 40.3 us -> 41.2 us
where the time goes in v1:
time: 840 us; the launch traced here: 838 us
  blocking collectives  313 us (37%)
  waiting for transfers between devices  304 us (36%)
  local copies, waits for them, and re-layouts  75.6 us (9%)
  starting transfers between devices  70.1 us (8%)
  matrix products  31.9 us (4%)
  other arithmetic  28.3 us (3%)
  between operations  14.7 us (2%)
    unnamed x1, blocking collectives  287 us
    all_gather x1, waiting for transfers between devices, on_device(): lax.all_gather(output_weight, 'tm', axis=0, tiled=True)  85.6 us
    all_gather x1, waiting for transfers between devices, on_device(): lax.all_gather(query_weight, 'tm', axis=0, tiled=True)  72.7 us
    all_gather x1, waiting for transfers between devices, on_device(): lax.all_gather(value_weight, 'tm', axis=0, tiled=True)  71.5 us
    all_gather x1, waiting for transfers between devices, on_device(): lax.all_gather(key_weight, 'tm', axis=0, tiled=True)  71.2 us
    unnamed x48, local copies, waits for them, and re-layouts  41.2 us
    all_gather x1, blocking collectives, gather_and_add(): pieces = lax.all_gather(x, name)  26 us
  transfers between devices with their start and end apart: 12, of which 4 were waited for; matrix products, arithmetic and copies ran while one was open for 14% of the time, Pallas kernels for 0%

profile of v1, /device:TPU:64, one launch (start us, length us, event | category | flops | bytes accessed | tf_op | source)
XLA Modules:
  0.0 837.5 jit_solution(13185301400653772636)
XLA Ops:
  12.6 85.6 %all-gather.17.cloned.1.call-done = bf16[64,10,1280]{2,1,0:T(8,128)(2,1)} async-done(((bf16[1,10,1280]{2,1,0:T(8,128)(2,1)}), bf16[64,10,1280]{2,1,0:T(8,128)(2,1)}) %all-gather.17.cloned.1.call-update) | async-done | bytes 1638416 | tf_op jit(solution)/shard_map/all_gather | solution.py:112
  102.6 6.7 all-to-all-start.4
  110.7 71.2 %all-gather.15.cloned.1.call-done = bf16[64,20,640]{2,1,0:T(8,128)(2,1)} async-done(((bf16[1,20,640]{2,1,0:T(8,128)(2,1)}), bf16[64,20,640]{2,1,0:T(8,128)(2,1)}) %all-gather.15.cloned.1.call-update) | async-done | bytes 1638416 | tf_op jit(solution)/shard_map/all_gather | solution.py:110
  185.9 7.0 all-to-all-start.2
  192.9 72.7 %all-gather.13.cloned.1.call-done = bf16[64,20,640]{2,1,0:T(8,128)(2,1)} async-done(((bf16[1,20,640]{2,1,0:T(8,128)(2,1)}), bf16[64,20,640]{2,1,0:T(8,128)(2,1)}) %all-gather.13.cloned.1.call-update) | async-done | bytes 1638416 | tf_op jit(solution)/shard_map/all_gather | solution.py:109
  270.7 7.0 all-to-all-start.1
  277.8 71.5 %all-gather.11.cloned.1.call-done = bf16[64,20,640]{2,1,0:T(8,128)(2,1)} async-done(((bf16[1,20,640]{2,1,0:T(8,128)(2,1)}), bf16[64,20,640]{2,1,0:T(8,128)(2,1)}) %all-gather.11.cloned.1.call-update) | async-done | bytes 1638416 | tf_op jit(solution)/shard_map/all_gather | solution.py:111
  349.3 3.6 reshape.311
  364.3 7.0 all-to-all-start
  375.5 2.9 fusion.43
  387.9 10.7 %all-to-all-start.7 = ((bf16[64,2,960]{2,1,0:T(2,128)(2,1)}), bf16[64,2,960]{2,1,0:T(2,128)(2,1)}, u32[]{:S(2)}, u32[]{:S(2)}) async-start(bf16[64,2,960]{2,1,0:T(2,128)(2,1)} %reshape.332), calls=%async_computation.7 | async-start | bytes 524288 | tf_op jit(solution)/shard_map/all_to_all | solution.py:156
  411.6 10.5 %all-to-all-start.3 = ((bf16[64,2,960]{2,1,0:T(2,128)(2,1)}), bf16[64,2,960]{2,1,0:T(2,128)(2,1)}, u32[]{:S(2)}, u32[]{:S(2)}) async-start(bf16[64,2,960]{2,1,0:T(2,128)(2,1)} %reshape.326), calls=%async_computation.3 | async-start | bytes 524288 | tf_op jit(solution)/shard_map/all_to_all | solution.py:132
  424.7 4.3 fusion.19
  435.3 10.5 %all-to-all-start.6 = ((bf16[64,2,960]{2,1,0:T(2,128)(2,1)}), bf16[64,2,960]{2,1,0:T(2,128)(2,1)}, u32[]{:S(2)}, u32[]{:S(2)}) async-start(bf16[64,2,960]{2,1,0:T(2,128)(2,1)} %reshape.330), calls=%async_computation.6 | async-start | bytes 524288 | tf_op jit(solution)/shard_map/all_to_all | solution.py:155
  447.8 4.4 fusion.16
  461.3 3.1 reduce.14
  470.7 3.1 reduce.11
  477.2 10.5 %all-to-all-start.5 = ((bf16[64,2,960]{2,1,0:T(2,128)(2,1)}), bf16[64,2,960]{2,1,0:T(2,128)(2,1)}, u32[]{:S(2)}, u32[]{:S(2)}) async-start(bf16[64,2,960]{2,1,0:T(2,128)(2,1)} %reshape.328), calls=%async_computation.5 | async-start | bytes 524288 | tf_op jit(solution)/shard_map/all_to_all | solution.py:154
  487.7 2.9 reshape.331
  490.6 3.1 reduce.13
  497.1 3.0 fusion.2
  505.3 3.1 reduce.12
  514.9 287.3 %all-reduce.2 = bf16[640,1280]{1,0:T(8,128)(2,1)} all-reduce(f32[640,1280]{1,0:T(8,128)} %fusion.46), channel_id=3, replica_groups=mesh['tm'=64,'dp'=8] {'tm'}, use_global_device_ids=true, to_apply=%region_7.8.clone | all-reduce | flops 819200 | bytes 4915200
  803.0 26.0 %all-gather.5 = bf16[8,10,1280]{2,1,0:T(8,128)(2,1)S(1)} all-gather(bf16[1,10,1280]{2,1,0:T(8,128)(2,1)S(1)} %fusion.35), channel_id=2, replica_groups=mesh['tm'=64,'dp'=8] {'dp'}, dimensions={0}, use_global_device_ids=true | all-gather | bytes 230400 | tf_op jit(solution)/shard_map/all_gather | solution.py:12
  (113 shorter events, 105.2 us)
Async XLA Ops:
  7.2 185.7 %copy-start = (s32[1,192,64]{1,2,0:T(8,128)S(1)}, s32[1,192,64]{1,2,0:T(8,128)}, u32[]{:S(2)}) copy-start(s32[1,192,64]{1,2,0:T(8,128)} %param.9) | copy-start | bytes 147460
  7.2 91.1 %all-gather.17.cloned.1.call-start = ((), (), s32[]{:S(2)}) async-start(), calls=%async_computation.11 | async-start | bytes 2662400 | tf_op jit(solution)/shard_map/all_gather | solution.py:112
  7.9 174.0 %all-gather.15.cloned.1.call-start = ((), (), s32[]{:S(2)}) async-start(), calls=%async_computation.10 | async-start | bytes 1996800 | tf_op jit(solution)/shard_map/all_gather | solution.py:110
  8.7 257.0 %all-gather.13.cloned.1.call-start = ((), (), s32[]{:S(2)}) async-start(), calls=%async_computation.9 | async-start | bytes 1996800 | tf_op jit(solution)/shard_map/all_gather | solution.py:109
  9.4 339.9 %all-gather.11.cloned.1.call-start = ((), (), s32[]{:S(2)}) async-start(), calls=%async_computation.8 | async-start | bytes 1996800 | tf_op jit(solution)/shard_map/all_gather | solution.py:111
  12.6 88.3 %copy-start.6 = (bf16[1,3,64,1280]{3,2,1,0:T(8,128)(2,1)S(1)}, bf16[1,3,64,1280]{3,2,1,0:T(8,128)(2,1)}, u32[]{:S(2)}) copy-start(bf16[1,3,64,1280]{3,2,1,0:T(8,128)(2,1)} %param.10) | copy-start | bytes 1474564
  101.0 8.4 %copy-start.3 = (bf16[1,3,64,1280]{3,2,1,0:T(8,128)(2,1)S(1)}, bf16[1,3,64,1280]{3,2,1,0:T(8,128)(2,1)}, u32[]{:S(2)}) copy-start(bf16[1,3,64,1280]{3,2,1,0:T(8,128)(2,1)} %param.8) | copy-start | bytes 1474564
  101.0 8.4 copy-start.14
  102.6 83.2 %all-to-all-start.4 = ((bf16[3,64,640]{2,0,1:T(4,128)(2,1)}), bf16[3,64,640]{2,0,1:T(4,128)(2,1)S(1)}, u32[]{:S(2)}, u32[]{:S(2)}) async-start(bf16[3,64,640]{2,0,1:T(4,128)(2,1)} %copy.52), calls=%async_computation.4 | async-start | bytes 655360 | tf_op jit(solution)/shard_map/all_to_all | solution.py:149
  110.7 73.6 %copy-start.5 = (bf16[192,1280]{1,0:T(8,128)(2,1)}, bf16[192,1280]{1,0:T(8,128)(2,1)S(1)}, u32[]{:S(2)}) copy-start(bf16[192,1280]{1,0:T(8,128)(2,1)S(1)} %get-tuple-element.6) | copy-start | bytes 1474564
  185.9 7.1 copy-start.11
  185.9 84.8 %all-to-all-start.2 = ((bf16[3,64,640]{2,0,1:T(4,128)(2,1)}), bf16[3,64,640]{2,0,1:T(4,128)(2,1)}, u32[]{:S(2)}, u32[]{:S(2)}) async-start(bf16[3,64,640]{2,0,1:T(4,128)(2,1)} %copy.45), calls=%async_computation.2 | async-start | bytes 655360 | tf_op jit(solution)/shard_map/all_to_all | solution.py:128
  270.7 93.7 %all-to-all-start.1 = ((bf16[3,64,640]{2,0,1:T(4,128)(2,1)}), bf16[3,64,640]{2,0,1:T(4,128)(2,1)}, u32[]{:S(2)}, u32[]{:S(2)}) async-start(bf16[3,64,640]{2,0,1:T(4,128)(2,1)} %copy.44), calls=%async_computation.1 | async-start | bytes 655360 | tf_op jit(solution)/shard_map/all_to_all | solution.py:127
  364.3 23.6 %all-to-all-start = ((bf16[3,64,640]{2,0,1:T(4,128)(2,1)}), bf16[3,64,640]{2,0,1:T(4,128)(2,1)}, u32[]{:S(2)}, u32[]{:S(2)}) async-start(bf16[3,64,640]{2,0,1:T(4,128)(2,1)} %copy.43), calls=%async_computation | async-start | bytes 655360 | tf_op jit(solution)/shard_map/all_to_all | solution.py:129
  387.9 23.7 %all-to-all-start.7 = ((bf16[64,2,960]{2,1,0:T(2,128)(2,1)}), bf16[64,2,960]{2,1,0:T(2,128)(2,1)}, u32[]{:S(2)}, u32[]{:S(2)}) async-start(bf16[64,2,960]{2,1,0:T(2,128)(2,1)} %reshape.332), calls=%async_computation.7 | async-start | bytes 524288 | tf_op jit(solution)/shard_map/all_to_all | solution.py:156
  411.6 23.8 %all-to-all-start.3 = ((bf16[64,2,960]{2,1,0:T(2,128)(2,1)}), bf16[64,2,960]{2,1,0:T(2,128)(2,1)}, u32[]{:S(2)}, u32[]{:S(2)}) async-start(bf16[64,2,960]{2,1,0:T(2,128)(2,1)} %reshape.326), calls=%async_computation.3 | async-start | bytes 524288 | tf_op jit(solution)/shard_map/all_to_all | solution.py:132
  435.3 41.9 %all-to-all-start.6 = ((bf16[64,2,960]{2,1,0:T(2,128)(2,1)}), bf16[64,2,960]{2,1,0:T(2,128)(2,1)}, u32[]{:S(2)}, u32[]{:S(2)}) async-start(bf16[64,2,960]{2,1,0:T(2,128)(2,1)} %reshape.330), calls=%async_computation.6 | async-start | bytes 524288 | tf_op jit(solution)/shard_map/all_to_all | solution.py:155
  477.2 25.3 %all-to-all-start.5 = ((bf16[64,2,960]{2,1,0:T(2,128)(2,1)}), bf16[64,2,960]{2,1,0:T(2,128)(2,1)}, u32[]{:S(2)}, u32[]{:S(2)}) async-start(bf16[64,2,960]{2,1,0:T(2,128)(2,1)} %reshape.328), calls=%async_computation.5 | async-start | bytes 524288 | tf_op jit(solution)/shard_map/all_to_all | solution.py:154
  497.1 3.0 copy-start.7
  497.1 3.0 copy-start.10
  512.1 1.7 copy-start.9
  512.1 1.7 copy-start.12
  514.9 314.9 %copy-start.4 = (bf16[1,3,64,1280]{3,2,1,0:T(8,128)(2,1)S(1)}, bf16[1,3,64,1280]{3,2,1,0:T(8,128)(2,1)}, u32[]{:S(2)}) copy-start(bf16[1,3,64,1280]{3,2,1,0:T(8,128)(2,1)} %param.8) | copy-start | bytes 1474564
  514.9 314.9 %copy-start.8 = (bf16[1,3,64,1280]{3,2,1,0:T(8,128)(2,1)S(1)}, bf16[1,3,64,1280]{3,2,1,0:T(8,128)(2,1)}, u32[]{:S(2)}) copy-start(bf16[1,3,64,1280]{3,2,1,0:T(8,128)(2,1)} %param.10) | copy-start | bytes 1474564
  (3 other events, 4.0 us)
Sparse Core Ops, SparseCore 0:
  11.3 86.8 all-gather.16
  101.5 80.3 all-gather.14
  185.2 80.4 all-gather.12
  268.8 80.4 all-gather.10
